TPU v7x, 32 devices: a whole 2x2x4 slice. The times are simulated.
32 devices in a mesh: dp: 2 (over x), ctx: 16 (over z, y, core).
Axes of the slice: x: 2, y: 2, z: 4, core: 2. Of those that a mesh axis runs over, the one named last changes fastest.
Arguments:
- features: bfloat16 [2, 2048, 1536], P('dp', 'ctx'), may hold values from -500 to 500
- gain: float32 [1536], replicated, may hold values from 0.1 to 1.9
- conv_weight: bfloat16 [5, 1536, 768], replicated, may hold values from -0.0625 to 0.0625
- cotangent: bfloat16 [2, 2048, 768], P('dp', 'ctx'), may hold values from -15 to 15
Outputs:
- convolved: bfloat16 [2, 2048, 768], P('dp', 'ctx')
- input_grad: bfloat16 [2, 2048, 1536], P('dp', 'ctx')
- gain_grad: float32 [1536], replicated
All inputs are finite; a program needn't handle non-finite values.
Results may differ from a plain program's by a relative error of at most 0.0054.
Values may be sent and summed in bfloat16 or wider, within the bound.
A program may use at most 64 MiB of HBM per device.

v0:
```python
import math
import jax
import jax.numpy as jnp
from jax import lax
from jax.sharding import PartitionSpec as P

KERNEL_TAPS = 5
EPS = 1e-06


def shifted(block, axis, distance):
    devices = range(lax.axis_size(axis))
    route = [(i - distance, i) for i in devices if i - distance in devices]
    return lax.ppermute(block, axis, route)


def activate(values):
    return jax.nn.gelu(values, approximate=True)


def flip_channels(values):
    return values[:, :, ::-1]


def taps_ahead(values, shard_hops):
    pieces = []
    for tap_index in range(KERNEL_TAPS):
        if tap_index == KERNEL_TAPS // 2:
            pieces.append(values)
        else:
            pieces.append(shifted(values, "ctx", -(tap_index - KERNEL_TAPS // 2) * shard_hops))
    return pieces


def taps_behind(values, shard_hops):
    pieces = []
    for tap_index in range(KERNEL_TAPS):
        if tap_index == KERNEL_TAPS // 2:
            pieces.append(values)
        else:
            pieces.append(shifted(values, "ctx", (tap_index - KERNEL_TAPS // 2) * shard_hops))
    return pieces


def apply_forward(pieces, weight):
    lead = pieces[0].shape[0]
    middle = pieces[0].shape[1]
    total = jnp.zeros((lead * middle, weight.shape[2]), jnp.float32)
    for tap_index in range(KERNEL_TAPS):
        flat_rows = pieces[tap_index].reshape(lead * middle, pieces[tap_index].shape[2])
        total = total + jnp.dot(flat_rows, weight[tap_index], preferred_element_type=jnp.float32)
    return total.reshape(lead, middle, weight.shape[2])


def apply_backward(pieces, weight):
    lead = pieces[0].shape[0]
    middle = pieces[0].shape[1]
    total = jnp.zeros((lead * middle, weight.shape[1]), jnp.float32)
    for tap_index in range(KERNEL_TAPS):
        flat_rows = pieces[tap_index].reshape(lead * middle, pieces[tap_index].shape[2])
        total = total + lax.dot_general(
            flat_rows,
            weight[tap_index],
            (((1,), (1,)), ((), ())),
            preferred_element_type=jnp.float32,
        )
    return total.reshape(lead, middle, weight.shape[1])


def per_device(features, gain, conv_weight, cotangent):
    shard_hops = lax.axis_size("ctx") // 8
    wide = features.astype(jnp.float32)
    inv_rms = lax.rsqrt(jnp.mean(wide * wide, axis=-1, keepdims=True) + EPS)
    normed = wide * inv_rms
    scaled = normed * gain
    hidden = activate(scaled).astype(jnp.bfloat16)
    ahead = taps_ahead(hidden, shard_hops)
    forward_term = apply_forward(ahead, conv_weight)
    flipped = [
        flip_channels(ahead[KERNEL_TAPS - 1 - tap_index]) for tap_index in range(KERNEL_TAPS)
    ]
    reverse_term = flip_channels(apply_forward(flipped, conv_weight).astype(jnp.bfloat16))
    convolved = (forward_term + reverse_term.astype(jnp.float32)).astype(jnp.bfloat16)
    behind = taps_behind(cotangent, shard_hops)
    back_forward = apply_backward(behind, conv_weight)
    flipped_grads = [
        flip_channels(behind[KERNEL_TAPS - 1 - tap_index]) for tap_index in range(KERNEL_TAPS)
    ]
    back_reverse = flip_channels(apply_backward(flipped_grads, conv_weight).astype(jnp.bfloat16))
    grad_hidden = back_forward + back_reverse.astype(jnp.float32)
    _, pullback = jax.vjp(activate, scaled)
    grad_scaled = pullback(grad_hidden)[0]
    partial_sum = jnp.sum(grad_scaled * normed, axis=(0, 1))
    summed = lax.psum(partial_sum, ("dp", "ctx"))
    total_rows = features.shape[0] * features.shape[1] * lax.axis_size("dp") * lax.axis_size("ctx")
    gain_grad = summed / math.sqrt(total_rows)
    grad_normed = grad_scaled * gain
    spread_term = jnp.mean(grad_normed * normed, axis=-1, keepdims=True)
    input_grad = (inv_rms * (grad_normed - normed * spread_term)).astype(jnp.bfloat16)
    return (convolved, input_grad, gain_grad)


def solution(mesh):
    return jax.shard_map(
        per_device,
        mesh=mesh,
        in_specs=(P("dp", "ctx", None), P(), P(), P("dp", "ctx", None)),
        out_specs=(P("dp", "ctx", None), P("dp", "ctx", None), P()),
        check_vma=False,
    )
```

profile of v0, /device:TPU:0, one launch (start us, length us, event | category | flops | bytes accessed | tf_op | source)
XLA Modules:
  0.0 152.5 jit_solution(12865565920787407074)
XLA Ops:
  0.6 4.9 %collective-permute-start.6 = (bf16[1,128,768]{2,1,0:T(8,128)(2,1)}, bf16[1,128,768]{2,1,0:T(8,128)(2,1)S(1)}, u32[]{:S(2)}, u32[]{:S(2)}) collective-permute-start(bf16[1,128,768]{2,1,0:T(8,128)(2,1)} %param.7), channel_id=1, source_target_pairs={{0,2},{1,3},{2,4},{3,5},{4,6},{5,7},{6,8},{7,9},{8,10},{9,11},{10,... | collective-permute-start | bytes 589832 | tf_op jit(solution)/shard_map/ppermute | solution.py:14
  5.5 3.5 %collective-permute-start.7 = (bf16[1,128,768]{2,1,0:T(8,128)(2,1)}, bf16[1,128,768]{2,1,0:T(8,128)(2,1)S(1)}, u32[]{:S(2)}, u32[]{:S(2)}) collective-permute-start(bf16[1,128,768]{2,1,0:T(8,128)(2,1)} %param.7), channel_id=1, source_target_pairs={{0,4},{1,5},{2,6},{3,7},{4,8},{5,9},{6,10},{7,11},{8,12},{9,13},{1... | collective-permute-start | bytes 589832 | tf_op jit(solution)/shard_map/ppermute | solution.py:14
  9.0 1.3 collective-permute-start.4
  11.6 2.7 %rev.39 = bf16[1,128,768]{2,1,0:T(8,128)(2,1)S(1)} reverse(bf16[1,128,768]{2,1,0:T(8,128)(2,1)} %param.7), dimensions={2} | reverse | bytes 393216 | tf_op jit(solution)/shard_map/rev | solution.py:22
  14.3 2.7 %fusion.23 = f32[128,1536]{1,0:T(8,128)S(1)} fusion(bf16[5,1536,768]{2,1,0:T(8,128)(2,1)} %param.6, bf16[1,128,768]{2,1,0:T(8,128)(2,1)} %param.7), kind=kOutput, calls=%fused_computation.27 | convolution fusion | flops 301989888 | bytes 3342336 | tf_op jit(solution)/shard_map/dot_general | solution.py:61
  17.0 2.6 %fusion.21 = f32[128,1536]{1,0:T(8,128)S(1)} fusion(bf16[5,1536,768]{2,1,0:T(8,128)(2,1)} %param.6, bf16[1,128,768]{2,1,0:T(8,128)(2,1)S(1)} %rev.39), kind=kOutput, calls=%fused_computation.25 | convolution fusion | flops 301989888 | bytes 3342336 | tf_op jit(solution)/shard_map/dot_general | solution.py:61
  21.4 2.5 %fusion.29 = f32[128,1536]{1,0:T(8,128)S(1)} fusion(bf16[5,1536,768]{2,1,0:T(8,128)(2,1)} %param.6, bf16[1,128,768]{2,1,0:T(8,128)(2,1)S(1)} %rev.38), kind=kOutput, calls=%fused_computation.33 | convolution fusion | flops 301989888 | bytes 3342336 | tf_op jit(solution)/shard_map/dot_general | solution.py:61
  24.6 2.2 %rev.37 = bf16[1,128,768]{2,1,0:T(8,128)(2,1)} reverse(bf16[1,128,768]{2,1,0:T(8,128)(2,1)S(1)} %collective-permute-done.7), dimensions={2} | reverse | bytes 393216 | tf_op jit(solution)/shard_map/rev | solution.py:22
  26.8 2.7 %fusion.1 = f32[128,1536]{1,0:T(8,128)S(1)} fusion(f32[128,1536]{1,0:T(8,128)S(1)} %fusion.21, f32[128,1536]{1,0:T(8,128)S(1)} %fusion.29, bf16[5,1536,768]{2,1,0:T(8,128)(2,1)} %param.6, bf16[1,128,768]{2,1,0:T(8,128)(2,1)} %rev.37), kind=kOutput, calls=%fused_computation.3 | convolution fusion | flops 302383104 | bytes 4915200 | tf_op jit(solution)/shard_map/dot_general | solution.py:61
  29.6 2.7 %rev.41 = bf16[1,128,768]{2,1,0:T(8,128)(2,1)S(1)} reverse(bf16[1,128,768]{2,1,0:T(8,128)(2,1)} %collective-permute-done.4), dimensions={2} | reverse | bytes 393216 | tf_op jit(solution)/shard_map/rev | solution.py:22
  32.3 2.6 %fusion.7 = f32[128,1536]{1,0:T(8,128)S(1)} fusion(bf16[5,1536,768]{2,1,0:T(8,128)(2,1)} %param.6, bf16[1,128,768]{2,1,0:T(8,128)(2,1)S(1)} %rev.41), kind=kOutput, calls=%fused_computation.11 | convolution fusion | flops 301989888 | bytes 3342336 | tf_op jit(solution)/shard_map/dot_general | solution.py:61
  34.9 2.7 %rev.40 = bf16[1,128,768]{2,1,0:T(8,128)(2,1)S(1)} reverse(bf16[1,128,768]{2,1,0:T(8,128)(2,1)} %collective-permute-done.5), dimensions={2} | reverse | bytes 393216 | tf_op jit(solution)/shard_map/rev | solution.py:22
  37.5 2.6 %fusion.6 = bf16[128,1536]{1,0:T(8,128)(2,1)S(1)} fusion(f32[128,1536]{1,0:T(8,128)S(1)} %fusion.7, f32[128,1536]{1,0:T(8,128)S(1)} %fusion.1, bf16[5,1536,768]{2,1,0:T(8,128)(2,1)} %param.6, bf16[1,128,768]{2,1,0:T(8,128)(2,1)S(1)} %rev.40), kind=kOutput, calls=%fused_computation.10 | convolution fusion | flops 302579712 | bytes 4521984 | tf_op jit(solution)/shard_map/dot_general | solution.py:61
  41.3 2.7 %fusion.31 = f32[128,1536]{1,0:T(8,128)S(1)} fusion(bf16[5,1536,768]{2,1,0:T(8,128)(2,1)} %param.6, bf16[1,128,768]{2,1,0:T(8,128)(2,1)} %collective-permute-done.5), kind=kOutput, calls=%fused_computation.35 | convolution fusion | flops 301989888 | bytes 3342336 | tf_op jit(solution)/shard_map/dot_general | solution.py:61
  44.0 2.5 %fusion.9 = f32[128,1536]{1,0:T(8,128)S(1)} fusion(bf16[5,1536,768]{2,1,0:T(8,128)(2,1)} %param.6, bf16[1,128,768]{2,1,0:T(8,128)(2,1)S(1)} %copy-done.2), kind=kOutput, calls=%fused_computation.13 | convolution fusion | flops 301989888 | bytes 3342336 | tf_op jit(solution)/shard_map/dot_general | solution.py:61
  46.5 2.7 %fusion.4 = f32[128,1536]{1,0:T(8,128)S(1)} fusion(f32[128,1536]{1,0:T(8,128)S(1)} %fusion.23, f32[128,1536]{1,0:T(8,128)S(1)} %fusion.31, bf16[5,1536,768]{2,1,0:T(8,128)(2,1)} %param.6, bf16[1,128,768]{2,1,0:T(8,128)(2,1)} %collective-permute-done.4), kind=kOutput, calls=%fused_computation.8 | convolution fusion | flops 302383104 | bytes 4915200 | tf_op jit(solution)/shard_map/dot_general | solution.py:61
  49.3 3.1 %fusion.115 = (f32[1536]{0:T(1024)S(1)}, f32[128]{0:T(128)S(1)}, f32[1,128,1536]{2,1,0:T(8,128)S(1)}) fusion(bf16[1,128,1536]{2,1,0:T(8,128)(2,1)S(1)} %copy-done, f32[128]{0:T(128)S(1)} %add_rsqrt_fusion, f32[1536]{0:T(1024)S(1)} %copy-done.5, bf16[128,1536]{1,0:T(8,128)(2,1)S(1)} %reverse.7, f32[128,1536]{1,0:T(8,128)S(1)} %fusion.9, ...), kind=kOutput, calls=%fused_computation.99 | convolution fusion | flops 308083072 | bytes 5714944 | tf_op jit(solution)/shard_map/dot_general | solution.py:61
  53.7 5.5 %collective-permute-start = (bf16[1,128,1536]{2,1,0:T(8,128)(2,1)S(1)}, bf16[1,128,1536]{2,1,0:T(8,128)(2,1)S(1)}, u32[]{:S(2)}, u32[]{:S(2)}) collective-permute-start(bf16[1,128,1536]{2,1,0:T(8,128)(2,1)S(1)} %get-tuple-element.6), channel_id=1, source_target_pairs={{0,4},{1,5},{2,6},{3,7},{4,8},{5,9},{6,10},{7,11},{8,12},{9,13},{1... | collective-permute-start | bytes 1179656 | tf_op jit(solution)/shard_map/ppermute | solution.py:14
  59.2 3.6 %collective-permute-start.1 = (bf16[1,128,1536]{2,1,0:T(8,128)(2,1)S(1)}, bf16[1,128,1536]{2,1,0:T(8,128)(2,1)S(1)}, u32[]{:S(2)}, u32[]{:S(2)}) collective-permute-start(bf16[1,128,1536]{2,1,0:T(8,128)(2,1)S(1)} %get-tuple-element.6), channel_id=1, source_target_pairs={{0,2},{1,3},{2,4},{3,5},{4,6},{5,7},{6,8},{7,9},{8,10},{9,11},{10,... | collective-permute-start | bytes 1179656 | tf_op jit(solution)/shard_map/ppermute | solution.py:14
  66.6 2.1 %fusion.27 = f32[128,768]{1,0:T(8,128)S(1)} fusion(bf16[5,1536,768]{2,1,0:T(8,128)(2,1)} %param.6, bf16[1,128,1536]{2,1,0:T(8,128)(2,1)S(1)} %get-tuple-element.6), kind=kOutput, calls=%fused_computation.31 | convolution fusion | flops 301989888 | bytes 3145728 | tf_op jit(solution)/shard_map/dot_general | solution.py:51
  68.8 47.5 %psum.7 = f32[1536]{0:T(1024)S(1)} all-reduce(f32[1536]{0:T(1024)S(1)} %get-tuple-element.3), channel_id=1, replica_groups=mesh['dp'=2,'ctx'=16] {'dp','ctx'}, use_global_device_ids=true, to_apply=%region_3.0 | all-reduce | flops 1536 | bytes 12288 | tf_op jit(solution)/shard_map/psum | solution.py:94
  116.3 2.1 %fusion.25 = f32[128,768]{1,0:T(8,128)S(1)} fusion(bf16[5,1536,768]{2,1,0:T(8,128)(2,1)} %param.6, bf16[1,128,1536]{2,1,0:T(8,128)(2,1)S(1)} %rev.34), kind=kOutput, calls=%fused_computation.29 | convolution fusion | flops 301989888 | bytes 3145728 | tf_op jit(solution)/shard_map/dot_general | solution.py:51
  120.3 2.1 %fusion.11 = f32[128,768]{1,0:T(8,128)S(1)} fusion(bf16[5,1536,768]{2,1,0:T(8,128)(2,1)} %param.6, bf16[1,128,1536]{2,1,0:T(8,128)(2,1)S(1)} %rev.36), kind=kOutput, calls=%fused_computation.15 | convolution fusion | flops 301989888 | bytes 3145728 | tf_op jit(solution)/shard_map/dot_general | solution.py:51
  123.7 2.1 %fusion.17 = f32[128,768]{1,0:T(8,128)S(1)} fusion(bf16[5,1536,768]{2,1,0:T(8,128)(2,1)} %param.6, bf16[1,128,1536]{2,1,0:T(8,128)(2,1)S(1)} %rev.35), kind=kOutput, calls=%fused_computation.21 | convolution fusion | flops 301989888 | bytes 3145728 | tf_op jit(solution)/shard_map/dot_general | solution.py:51
  125.9 6.7 %rev.33 = bf16[1,128,1536]{2,1,0:T(8,128)(2,1)} reverse(bf16[1,128,1536]{2,1,0:T(8,128)(2,1)} %collective-permute-done.2), dimensions={2} | reverse | bytes 786432 | tf_op jit(solution)/shard_map/rev | solution.py:22
  132.6 2.3 %fusion.33 = f32[128,768]{1,0:T(8,128)S(1)} fusion(bf16[5,1536,768]{2,1,0:T(8,128)(2,1)} %param.6, bf16[1,128,1536]{2,1,0:T(8,128)(2,1)} %rev.33), kind=kOutput, calls=%fused_computation.37 | convolution fusion | flops 301989888 | bytes 3145728 | tf_op jit(solution)/shard_map/dot_general | solution.py:51
  134.9 5.2 %rev.32 = bf16[1,128,1536]{2,1,0:T(8,128)(2,1)S(1)} reverse(bf16[1,128,1536]{2,1,0:T(8,128)(2,1)} %collective-permute-done.3), dimensions={2} | reverse | bytes 786432 | tf_op jit(solution)/shard_map/rev | solution.py:22
  140.1 2.2 %fusion.90 = bf16[128,768]{1,0:T(8,128)(2,1)S(1)} fusion(f32[128,768]{1,0:T(8,128)S(1)} %fusion.11, f32[128,768]{1,0:T(8,128)S(1)} %fusion.17, f32[128,768]{1,0:T(8,128)S(1)} %fusion.25, f32[128,768]{1,0:T(8,128)S(1)} %fusion.33, bf16[5,1536,768]{2,1,0:T(8,128)(2,1)} %param.6, bf16[1,128,1536]{2,1,0:T(8,128)(2,1)S(1)} %rev.32), kind=kOutput, calls=%fused_computation.76 | convolution fusion | flops 302481408 | bytes 4521984 | tf_op jit(solution)/shard_map/dot_general | solution.py:51
  142.9 2.3 %fusion.13 = f32[128,768]{1,0:T(8,128)S(1)} fusion(bf16[5,1536,768]{2,1,0:T(8,128)(2,1)} %param.6, bf16[1,128,1536]{2,1,0:T(8,128)(2,1)} %collective-permute-done.3), kind=kOutput, calls=%fused_computation.17 | convolution fusion | flops 301989888 | bytes 3145728 | tf_op jit(solution)/shard_map/dot_general | solution.py:51
  145.2 2.3 %fusion.19 = f32[128,768]{1,0:T(8,128)S(1)} fusion(bf16[5,1536,768]{2,1,0:T(8,128)(2,1)} %param.6, bf16[1,128,1536]{2,1,0:T(8,128)(2,1)} %collective-permute-done.2), kind=kOutput, calls=%fused_computation.23 | convolution fusion | flops 301989888 | bytes 3145728 | tf_op jit(solution)/shard_map/dot_general | solution.py:51
  147.5 2.1 %fusion.35 = f32[128,768]{1,0:T(8,128)S(1)} fusion(bf16[5,1536,768]{2,1,0:T(8,128)(2,1)} %param.6, bf16[1,128,1536]{2,1,0:T(8,128)(2,1)S(1)} %collective-permute-done.1), kind=kOutput, calls=%fused_computation.39 | convolution fusion | flops 301989888 | bytes 3145728 | tf_op jit(solution)/shard_map/dot_general | solution.py:51
  149.6 2.9 %fusion.96 = bf16[1,128,768]{2,1,0:T(8,128)(2,1)} fusion(f32[128,768]{1,0:T(8,128)S(1)} %fusion.13, f32[128,768]{1,0:T(8,128)S(1)} %fusion.19, f32[128,768]{1,0:T(8,128)S(1)} %fusion.27, f32[128,768]{1,0:T(8,128)S(1)} %fusion.35, bf16[5,1536,768]{2,1,0:T(8,128)(2,1)} %param.6, bf16[1,128,1536]{2,1,0:T(8,128)(2,1)S(1)} %collective-permute-done, ...), kind=kOutput, calls=%fused_computation.78 | convolution fusion | flops 302678016 | bytes 4718592 | tf_op jit(solution)/shard_map/dot_general | solution.py:51
  (34 shorter events, 13.7 us)
Async XLA Ops:
  0.6 20.1 %collective-permute-start.6 = (bf16[1,128,768]{2,1,0:T(8,128)(2,1)}, bf16[1,128,768]{2,1,0:T(8,128)(2,1)S(1)}, u32[]{:S(2)}, u32[]{:S(2)}) collective-permute-start(bf16[1,128,768]{2,1,0:T(8,128)(2,1)} %param.7), channel_id=1, source_target_pairs={{0,2},{1,3},{2,4},{3,5},{4,6},{5,7},{6,8},{7,9},{8,10},{9,11},{10,... | collective-permute-start | bytes 589832 | tf_op jit(solution)/shard_map/ppermute | solution.py:14
  5.5 18.4 %collective-permute-start.7 = (bf16[1,128,768]{2,1,0:T(8,128)(2,1)}, bf16[1,128,768]{2,1,0:T(8,128)(2,1)S(1)}, u32[]{:S(2)}, u32[]{:S(2)}) collective-permute-start(bf16[1,128,768]{2,1,0:T(8,128)(2,1)} %param.7), channel_id=1, source_target_pairs={{0,4},{1,5},{2,6},{3,7},{4,8},{5,9},{6,10},{7,11},{8,12},{9,13},{1... | collective-permute-start | bytes 589832 | tf_op jit(solution)/shard_map/ppermute | solution.py:14
  9.0 20.5 %collective-permute-start.4 = (bf16[1,128,768]{2,1,0:T(8,128)(2,1)}, bf16[1,128,768]{2,1,0:T(8,128)(2,1)}, u32[]{:S(2)}, u32[]{:S(2)}) collective-permute-start(bf16[1,128,768]{2,1,0:T(8,128)(2,1)} %param.7), channel_id=1, source_target_pairs={{4,0},{5,1},{6,2},{7,3},{8,4},{9,5},{10,6},{11,7},{12,8},{13,9},{1... | collective-permute-start | bytes 589832 | tf_op jit(solution)/shard_map/ppermute | solution.py:14
  10.3 24.5 %collective-permute-start.5 = (bf16[1,128,768]{2,1,0:T(8,128)(2,1)}, bf16[1,128,768]{2,1,0:T(8,128)(2,1)}, u32[]{:S(2)}, u32[]{:S(2)}) collective-permute-start(bf16[1,128,768]{2,1,0:T(8,128)(2,1)} %param.7), channel_id=1, source_target_pairs={{2,0},{3,1},{4,2},{5,3},{6,4},{7,5},{8,6},{9,7},{10,8},{11,9},{12,... | collective-permute-start | bytes 589832 | tf_op jit(solution)/shard_map/ppermute | solution.py:14
  20.7 3.2 %copy-start.3 = (bf16[1,128,768]{2,1,0:T(8,128)(2,1)}, bf16[1,128,768]{2,1,0:T(8,128)(2,1)S(1)}, u32[]{:S(2)}) copy-start(bf16[1,128,768]{2,1,0:T(8,128)(2,1)S(1)} %collective-permute-done.6) | copy-start | bytes 589828
  23.9 0.7 copy-start.1
  26.8 22.4 %copy-start = (bf16[1,128,1536]{2,1,0:T(8,128)(2,1)S(1)}, bf16[1,128,1536]{2,1,0:T(8,128)(2,1)}, u32[]{:S(2)}) copy-start(bf16[1,128,1536]{2,1,0:T(8,128)(2,1)} %param.4) | copy-start | bytes 1179652
  26.8 22.4 %copy-start.5 = (f32[1536]{0:T(1024)S(1)}, f32[1536]{0:T(1024)}, u32[]{:S(2)}) copy-start(f32[1536]{0:T(1024)} %param.5) | copy-start | bytes 18436
  29.6 14.4 %copy-start.2 = (bf16[1,128,768]{2,1,0:T(8,128)(2,1)S(1)}, bf16[1,128,768]{2,1,0:T(8,128)(2,1)}, u32[]{:S(2)}) copy-start(bf16[1,128,768]{2,1,0:T(8,128)(2,1)} %copy-done.1) | copy-start | bytes 589828
  40.1 9.2 %copy-start.4 = (bf16[1,128,768]{2,1,0:T(8,128)(2,1)S(1)}, bf16[1,128,768]{2,1,0:T(8,128)(2,1)}, u32[]{:S(2)}) copy-start(bf16[1,128,768]{2,1,0:T(8,128)(2,1)} %copy-done.3) | copy-start | bytes 589828
  53.7 65.4 %collective-permute-start = (bf16[1,128,1536]{2,1,0:T(8,128)(2,1)S(1)}, bf16[1,128,1536]{2,1,0:T(8,128)(2,1)S(1)}, u32[]{:S(2)}, u32[]{:S(2)}) collective-permute-start(bf16[1,128,1536]{2,1,0:T(8,128)(2,1)S(1)} %get-tuple-element.6), channel_id=1, source_target_pairs={{0,4},{1,5},{2,6},{3,7},{4,8},{5,9},{6,10},{7,11},{8,12},{9,13},{1... | collective-permute-start | bytes 1179656 | tf_op jit(solution)/shard_map/ppermute | solution.py:14
  59.2 63.3 %collective-permute-start.1 = (bf16[1,128,1536]{2,1,0:T(8,128)(2,1)S(1)}, bf16[1,128,1536]{2,1,0:T(8,128)(2,1)S(1)}, u32[]{:S(2)}, u32[]{:S(2)}) collective-permute-start(bf16[1,128,1536]{2,1,0:T(8,128)(2,1)S(1)} %get-tuple-element.6), channel_id=1, source_target_pairs={{0,2},{1,3},{2,4},{3,5},{4,6},{5,7},{6,8},{7,9},{8,10},{9,11},{10,... | collective-permute-start | bytes 1179656 | tf_op jit(solution)/shard_map/ppermute | solution.py:14
  62.8 63.0 %collective-permute-start.2 = (bf16[1,128,1536]{2,1,0:T(8,128)(2,1)S(1)}, bf16[1,128,1536]{2,1,0:T(8,128)(2,1)}, u32[]{:S(2)}, u32[]{:S(2)}) collective-permute-start(bf16[1,128,1536]{2,1,0:T(8,128)(2,1)S(1)} %get-tuple-element.6), channel_id=1, source_target_pairs={{2,0},{3,1},{4,2},{5,3},{6,4},{7,5},{8,6},{9,7},{10,8},{11,9},{12,... | collective-permute-start | bytes 1179656 | tf_op jit(solution)/shard_map/ppermute | solution.py:14
  64.1 70.7 %collective-permute-start.3 = (bf16[1,128,1536]{2,1,0:T(8,128)(2,1)S(1)}, bf16[1,128,1536]{2,1,0:T(8,128)(2,1)}, u32[]{:S(2)}, u32[]{:S(2)}) collective-permute-start(bf16[1,128,1536]{2,1,0:T(8,128)(2,1)S(1)} %get-tuple-element.6), channel_id=1, source_target_pairs={{4,0},{5,1},{6,2},{7,3},{8,4},{9,5},{10,6},{11,7},{12,8},{13,9},{1... | collective-permute-start | bytes 1179656 | tf_op jit(solution)/shard_map/ppermute | solution.py:14
where the time goes:
time: 155 us; the launch traced here: 153 us
  matrix products  49.2 us (32%)
  blocking collectives  47.5 us (31%)
  local copies, waits for them, and re-layouts  28.9 us (19%)
  starting transfers between devices  22.7 us (15%)
  other arithmetic  3.03 us (2%)
    psum x1, blocking collectives, per_device(): summed = lax.psum(partial_sum, ('dp', 'ctx'))  47.5 us
    dot_general x10, matrix products, apply_backward(): lax.dot_general(flat_rows, weight[tap_index], (((1,), (1,)), ((), ())), p...  26.6 us
    rev x10, local copies, waits for them, and re-layouts, flip_channels(): return values[:, :, ::-1]  26.4 us
    ppermute x8, starting transfers between devices, shifted(): return lax.ppermute(block, axis, route)  22.7 us
    dot_general x10, matrix products, apply_forward(): jnp.dot(flat_rows, weight[tap_index], preferred_element_type=jnp.float32)  22.6 us
  transfers between devices with their start and end apart: 8, of which 0 were waited for; matrix products, arithmetic and copies ran while one was open for 29% of the time, Pallas kernels for 0%

commit v1 on v0

--- a/solution.py
+++ b/solution.py
@@ -6,6 +6,14 @@
 
 KERNEL_TAPS = 5
 EPS = 1e-06
+
+
+def _change_chains(own_rows):
+    net_axis = "dp"
+    shard_axis = "ctx"
+    for w in (shard_axis, net_axis):
+        own_rows = lax.psum(own_rows, w)
+    return own_rows
 
 
 def shifted(block, axis, distance):
@@ -91,7 +99,7 @@
     _, pullback = jax.vjp(activate, scaled)
     grad_scaled = pullback(grad_hidden)[0]
     partial_sum = jnp.sum(grad_scaled * normed, axis=(0, 1))
-    summed = lax.psum(partial_sum, ("dp", "ctx"))
+    summed = _change_chains(partial_sum)
     total_rows = features.shape[0] * features.shape[1] * lax.axis_size("dp") * lax.axis_size("ctx")
     gain_grad = summed / math.sqrt(total_rows)
     grad_normed = grad_scaled * gain

time: 155 us -> 149 us (0.961)
  blocking collectives: 47.5 us -> 40.9 us
    psum x1 -> x2, blocking collectives: 47.5 us -> 40.9 us  [_change_chains(): own_rows = lax.psum(own_rows, w)]
  transfers between devices with their start and end apart: 8 -> 8, of which waited for: 0 -> 0; matrix products, arithmetic and copies ran while one was open for 29% -> 30% of each run, Pallas kernels for 0% -> 0%
where the time goes in v1:
time: 149 us; the launch traced here: 146 us
  matrix products  49.2 us (33%)
  blocking collectives  40.9 us (27%)
  local copies, waits for them, and re-layouts  28.9 us (19%)
  starting transfers between devices  22.7 us (15%)
  other arithmetic  3.03 us (2%)
    psum x2, blocking collectives, _change_chains(): own_rows = lax.psum(own_rows, w)  40.9 us
    dot_general x10, matrix products, apply_backward(): lax.dot_general(flat_rows, weight[tap_index], (((1,), (1,)), ((), ())), p...  26.6 us
    rev x10, local copies, waits for them, and re-layouts, flip_channels(): return values[:, :, ::-1]  26.4 us
    ppermute x8, starting transfers between devices, shifted(): return lax.ppermute(block, axis, route)  22.7 us
    dot_general x10, matrix products, apply_forward(): jnp.dot(flat_rows, weight[tap_index], preferred_element_type=jnp.float32)  22.6 us
  transfers between devices with their start and end apart: 8, of which 0 were waited for; matrix products, arithmetic and copies ran while one was open for 30% of the time, Pallas kernels for 0%

profile of v1, /device:TPU:0, one launch (start us, length us, event | category | flops | bytes accessed | tf_op | source)
XLA Modules:
  0.0 145.9 jit_solution(11541098812302060212)
XLA Ops:
  0.6 4.9 %collective-permute-start.6 = (bf16[1,128,768]{2,1,0:T(8,128)(2,1)}, bf16[1,128,768]{2,1,0:T(8,128)(2,1)S(1)}, u32[]{:S(2)}, u32[]{:S(2)}) collective-permute-start(bf16[1,128,768]{2,1,0:T(8,128)(2,1)} %param.7), channel_id=1, source_target_pairs={{0,2},{1,3},{2,4},{3,5},{4,6},{5,7},{6,8},{7,9},{8,10},{9,11},{10,... | collective-permute-start | bytes 589832 | tf_op jit(solution)/shard_map/ppermute | solution.py:22
  5.5 3.5 %collective-permute-start.7 = (bf16[1,128,768]{2,1,0:T(8,128)(2,1)}, bf16[1,128,768]{2,1,0:T(8,128)(2,1)S(1)}, u32[]{:S(2)}, u32[]{:S(2)}) collective-permute-start(bf16[1,128,768]{2,1,0:T(8,128)(2,1)} %param.7), channel_id=1, source_target_pairs={{0,4},{1,5},{2,6},{3,7},{4,8},{5,9},{6,10},{7,11},{8,12},{9,13},{1... | collective-permute-start | bytes 589832 | tf_op jit(solution)/shard_map/ppermute | solution.py:22
  11.6 2.7 %rev.39 = bf16[1,128,768]{2,1,0:T(8,128)(2,1)S(1)} reverse(bf16[1,128,768]{2,1,0:T(8,128)(2,1)} %param.7), dimensions={2} | reverse | bytes 393216 | tf_op jit(solution)/shard_map/rev | solution.py:30
  14.3 2.7 %fusion.23 = f32[128,1536]{1,0:T(8,128)S(1)} fusion(bf16[5,1536,768]{2,1,0:T(8,128)(2,1)} %param.6, bf16[1,128,768]{2,1,0:T(8,128)(2,1)} %param.7), kind=kOutput, calls=%fused_computation.27 | convolution fusion | flops 301989888 | bytes 3342336 | tf_op jit(solution)/shard_map/dot_general | solution.py:69
  17.0 2.6 %fusion.21 = f32[128,1536]{1,0:T(8,128)S(1)} fusion(bf16[5,1536,768]{2,1,0:T(8,128)(2,1)} %param.6, bf16[1,128,768]{2,1,0:T(8,128)(2,1)S(1)} %rev.39), kind=kOutput, calls=%fused_computation.25 | convolution fusion | flops 301989888 | bytes 3342336 | tf_op jit(solution)/shard_map/dot_general | solution.py:69
  21.4 2.5 %fusion.29 = f32[128,1536]{1,0:T(8,128)S(1)} fusion(bf16[5,1536,768]{2,1,0:T(8,128)(2,1)} %param.6, bf16[1,128,768]{2,1,0:T(8,128)(2,1)S(1)} %rev.38), kind=kOutput, calls=%fused_computation.33 | convolution fusion | flops 301989888 | bytes 3342336 | tf_op jit(solution)/shard_map/dot_general | solution.py:69
  24.6 2.2 %rev.37 = bf16[1,128,768]{2,1,0:T(8,128)(2,1)} reverse(bf16[1,128,768]{2,1,0:T(8,128)(2,1)S(1)} %collective-permute-done.7), dimensions={2} | reverse | bytes 393216 | tf_op jit(solution)/shard_map/rev | solution.py:30
  26.8 2.7 %fusion.1 = f32[128,1536]{1,0:T(8,128)S(1)} fusion(f32[128,1536]{1,0:T(8,128)S(1)} %fusion.21, f32[128,1536]{1,0:T(8,128)S(1)} %fusion.29, bf16[5,1536,768]{2,1,0:T(8,128)(2,1)} %param.6, bf16[1,128,768]{2,1,0:T(8,128)(2,1)} %rev.37), kind=kOutput, calls=%fused_computation.3 | convolution fusion | flops 302383104 | bytes 4915200 | tf_op jit(solution)/shard_map/dot_general | solution.py:69
  29.6 2.7 %rev.41 = bf16[1,128,768]{2,1,0:T(8,128)(2,1)S(1)} reverse(bf16[1,128,768]{2,1,0:T(8,128)(2,1)} %collective-permute-done.4), dimensions={2} | reverse | bytes 393216 | tf_op jit(solution)/shard_map/rev | solution.py:30
  32.3 2.6 %fusion.7 = f32[128,1536]{1,0:T(8,128)S(1)} fusion(bf16[5,1536,768]{2,1,0:T(8,128)(2,1)} %param.6, bf16[1,128,768]{2,1,0:T(8,128)(2,1)S(1)} %rev.41), kind=kOutput, calls=%fused_computation.11 | convolution fusion | flops 301989888 | bytes 3342336 | tf_op jit(solution)/shard_map/dot_general | solution.py:69
  34.9 2.7 %rev.40 = bf16[1,128,768]{2,1,0:T(8,128)(2,1)S(1)} reverse(bf16[1,128,768]{2,1,0:T(8,128)(2,1)} %collective-permute-done.5), dimensions={2} | reverse | bytes 393216 | tf_op jit(solution)/shard_map/rev | solution.py:30
  37.5 2.6 %fusion.6 = bf16[128,1536]{1,0:T(8,128)(2,1)S(1)} fusion(f32[128,1536]{1,0:T(8,128)S(1)} %fusion.7, f32[128,1536]{1,0:T(8,128)S(1)} %fusion.1, bf16[5,1536,768]{2,1,0:T(8,128)(2,1)} %param.6, bf16[1,128,768]{2,1,0:T(8,128)(2,1)S(1)} %rev.40), kind=kOutput, calls=%fused_computation.10 | convolution fusion | flops 302579712 | bytes 4521984 | tf_op jit(solution)/shard_map/dot_general | solution.py:69
  41.3 2.7 %fusion.31 = f32[128,1536]{1,0:T(8,128)S(1)} fusion(bf16[5,1536,768]{2,1,0:T(8,128)(2,1)} %param.6, bf16[1,128,768]{2,1,0:T(8,128)(2,1)} %collective-permute-done.5), kind=kOutput, calls=%fused_computation.35 | convolution fusion | flops 301989888 | bytes 3342336 | tf_op jit(solution)/shard_map/dot_general | solution.py:69
  44.0 2.5 %fusion.9 = f32[128,1536]{1,0:T(8,128)S(1)} fusion(bf16[5,1536,768]{2,1,0:T(8,128)(2,1)} %param.6, bf16[1,128,768]{2,1,0:T(8,128)(2,1)S(1)} %copy-done.2), kind=kOutput, calls=%fused_computation.13 | convolution fusion | flops 301989888 | bytes 3342336 | tf_op jit(solution)/shard_map/dot_general | solution.py:69
  46.5 2.7 %fusion.4 = f32[128,1536]{1,0:T(8,128)S(1)} fusion(f32[128,1536]{1,0:T(8,128)S(1)} %fusion.23, f32[128,1536]{1,0:T(8,128)S(1)} %fusion.31, bf16[5,1536,768]{2,1,0:T(8,128)(2,1)} %param.6, bf16[1,128,768]{2,1,0:T(8,128)(2,1)} %collective-permute-done.4), kind=kOutput, calls=%fused_computation.8 | convolution fusion | flops 302383104 | bytes 4915200 | tf_op jit(solution)/shard_map/dot_general | solution.py:69
  49.3 3.1 %fusion.115 = (f32[1536]{0:T(1024)S(1)}, f32[128]{0:T(128)S(1)}, f32[1,128,1536]{2,1,0:T(8,128)S(1)}) fusion(bf16[1,128,1536]{2,1,0:T(8,128)(2,1)S(1)} %copy-done, f32[128]{0:T(128)S(1)} %add_rsqrt_fusion, f32[1536]{0:T(1024)S(1)} %copy-done.5, bf16[128,1536]{1,0:T(8,128)(2,1)S(1)} %reverse.7, f32[128,1536]{1,0:T(8,128)S(1)} %fusion.9, ...), kind=kOutput, calls=%fused_computation.99 | convolution fusion | flops 308083072 | bytes 5714944 | tf_op jit(solution)/shard_map/dot_general | solution.py:69
  53.7 5.5 %collective-permute-start = (bf16[1,128,1536]{2,1,0:T(8,128)(2,1)S(1)}, bf16[1,128,1536]{2,1,0:T(8,128)(2,1)S(1)}, u32[]{:S(2)}, u32[]{:S(2)}) collective-permute-start(bf16[1,128,1536]{2,1,0:T(8,128)(2,1)S(1)} %get-tuple-element.6), channel_id=1, source_target_pairs={{0,4},{1,5},{2,6},{3,7},{4,8},{5,9},{6,10},{7,11},{8,12},{9,13},{1... | collective-permute-start | bytes 1179656 | tf_op jit(solution)/shard_map/ppermute | solution.py:22
  59.2 3.6 %collective-permute-start.1 = (bf16[1,128,1536]{2,1,0:T(8,128)(2,1)S(1)}, bf16[1,128,1536]{2,1,0:T(8,128)(2,1)S(1)}, u32[]{:S(2)}, u32[]{:S(2)}) collective-permute-start(bf16[1,128,1536]{2,1,0:T(8,128)(2,1)S(1)} %get-tuple-element.6), channel_id=1, source_target_pairs={{0,2},{1,3},{2,4},{3,5},{4,6},{5,7},{6,8},{7,9},{8,10},{9,11},{10,... | collective-permute-start | bytes 1179656 | tf_op jit(solution)/shard_map/ppermute | solution.py:22
  66.6 2.1 %fusion.27 = f32[128,768]{1,0:T(8,128)S(1)} fusion(bf16[5,1536,768]{2,1,0:T(8,128)(2,1)} %param.6, bf16[1,128,1536]{2,1,0:T(8,128)(2,1)S(1)} %get-tuple-element.6), kind=kOutput, calls=%fused_computation.31 | convolution fusion | flops 301989888 | bytes 3145728 | tf_op jit(solution)/shard_map/dot_general | solution.py:59
  68.8 35.9 %psum.14 = f32[1536]{0:T(1024)S(1)} all-reduce(f32[1536]{0:T(1024)S(1)} %get-tuple-element.3), channel_id=1, replica_groups=mesh['dp'=2,'ctx'=16] {'ctx'}, use_global_device_ids=true, to_apply=%region_3.0 | all-reduce | flops 1536 | bytes 12288 | tf_op jit(solution)/shard_map/psum | solution.py:15
  104.7 5.0 %psum.15 = f32[1536]{0:T(1024)S(1)} all-reduce(f32[1536]{0:T(1024)S(1)} %psum.14), channel_id=1, replica_groups=mesh['dp'=2,'ctx'=16] {'dp'}, use_global_device_ids=true, to_apply=%region_4.0 | all-reduce | flops 1536 | bytes 12288 | tf_op jit(solution)/shard_map/psum | solution.py:15
  109.7 2.1 %fusion.25 = f32[128,768]{1,0:T(8,128)S(1)} fusion(bf16[5,1536,768]{2,1,0:T(8,128)(2,1)} %param.6, bf16[1,128,1536]{2,1,0:T(8,128)(2,1)S(1)} %rev.34), kind=kOutput, calls=%fused_computation.29 | convolution fusion | flops 301989888 | bytes 3145728 | tf_op jit(solution)/shard_map/dot_general | solution.py:59
  113.7 2.1 %fusion.11 = f32[128,768]{1,0:T(8,128)S(1)} fusion(bf16[5,1536,768]{2,1,0:T(8,128)(2,1)} %param.6, bf16[1,128,1536]{2,1,0:T(8,128)(2,1)S(1)} %rev.36), kind=kOutput, calls=%fused_computation.15 | convolution fusion | flops 301989888 | bytes 3145728 | tf_op jit(solution)/shard_map/dot_general | solution.py:59
  117.1 2.1 %fusion.17 = f32[128,768]{1,0:T(8,128)S(1)} fusion(bf16[5,1536,768]{2,1,0:T(8,128)(2,1)} %param.6, bf16[1,128,1536]{2,1,0:T(8,128)(2,1)S(1)} %rev.35), kind=kOutput, calls=%fused_computation.21 | convolution fusion | flops 301989888 | bytes 3145728 | tf_op jit(solution)/shard_map/dot_general | solution.py:59
  119.2 6.7 %rev.33 = bf16[1,128,1536]{2,1,0:T(8,128)(2,1)} reverse(bf16[1,128,1536]{2,1,0:T(8,128)(2,1)} %collective-permute-done.2), dimensions={2} | reverse | bytes 786432 | tf_op jit(solution)/shard_map/rev | solution.py:30
  125.9 2.3 %fusion.33 = f32[128,768]{1,0:T(8,128)S(1)} fusion(bf16[5,1536,768]{2,1,0:T(8,128)(2,1)} %param.6, bf16[1,128,1536]{2,1,0:T(8,128)(2,1)} %rev.33), kind=kOutput, calls=%fused_computation.37 | convolution fusion | flops 301989888 | bytes 3145728 | tf_op jit(solution)/shard_map/dot_general | solution.py:59
  128.2 5.2 %rev.32 = bf16[1,128,1536]{2,1,0:T(8,128)(2,1)S(1)} reverse(bf16[1,128,1536]{2,1,0:T(8,128)(2,1)} %collective-permute-done.3), dimensions={2} | reverse | bytes 786432 | tf_op jit(solution)/shard_map/rev | solution.py:30
  133.4 2.2 %fusion.90 = bf16[128,768]{1,0:T(8,128)(2,1)S(1)} fusion(f32[128,768]{1,0:T(8,128)S(1)} %fusion.11, f32[128,768]{1,0:T(8,128)S(1)} %fusion.17, f32[128,768]{1,0:T(8,128)S(1)} %fusion.25, f32[128,768]{1,0:T(8,128)S(1)} %fusion.33, bf16[5,1536,768]{2,1,0:T(8,128)(2,1)} %param.6, bf16[1,128,1536]{2,1,0:T(8,128)(2,1)S(1)} %rev.32), kind=kOutput, calls=%fused_computation.76 | convolution fusion | flops 302481408 | bytes 4521984 | tf_op jit(solution)/shard_map/dot_general | solution.py:59
  136.2 2.3 %fusion.13 = f32[128,768]{1,0:T(8,128)S(1)} fusion(bf16[5,1536,768]{2,1,0:T(8,128)(2,1)} %param.6, bf16[1,128,1536]{2,1,0:T(8,128)(2,1)} %collective-permute-done.3), kind=kOutput, calls=%fused_computation.17 | convolution fusion | flops 301989888 | bytes 3145728 | tf_op jit(solution)/shard_map/dot_general | solution.py:59
  138.5 2.3 %fusion.19 = f32[128,768]{1,0:T(8,128)S(1)} fusion(bf16[5,1536,768]{2,1,0:T(8,128)(2,1)} %param.6, bf16[1,128,1536]{2,1,0:T(8,128)(2,1)} %collective-permute-done.2), kind=kOutput, calls=%fused_computation.23 | convolution fusion | flops 301989888 | bytes 3145728 | tf_op jit(solution)/shard_map/dot_general | solution.py:59
  140.8 2.1 %fusion.35 = f32[128,768]{1,0:T(8,128)S(1)} fusion(bf16[5,1536,768]{2,1,0:T(8,128)(2,1)} %param.6, bf16[1,128,1536]{2,1,0:T(8,128)(2,1)S(1)} %collective-permute-done.1), kind=kOutput, calls=%fused_computation.39 | convolution fusion | flops 301989888 | bytes 3145728 | tf_op jit(solution)/shard_map/dot_general | solution.py:59
  143.0 2.9 %fusion.96 = bf16[1,128,768]{2,1,0:T(8,128)(2,1)} fusion(f32[128,768]{1,0:T(8,128)S(1)} %fusion.13, f32[128,768]{1,0:T(8,128)S(1)} %fusion.19, f32[128,768]{1,0:T(8,128)S(1)} %fusion.27, f32[128,768]{1,0:T(8,128)S(1)} %fusion.35, bf16[5,1536,768]{2,1,0:T(8,128)(2,1)} %param.6, bf16[1,128,1536]{2,1,0:T(8,128)(2,1)S(1)} %collective-permute-done, ...), kind=kOutput, calls=%fused_computation.78 | convolution fusion | flops 302678016 | bytes 4718592 | tf_op jit(solution)/shard_map/dot_general | solution.py:59
  (35 shorter events, 15.0 us)
Async XLA Ops:
  0.6 20.1 %collective-permute-start.6 = (bf16[1,128,768]{2,1,0:T(8,128)(2,1)}, bf16[1,128,768]{2,1,0:T(8,128)(2,1)S(1)}, u32[]{:S(2)}, u32[]{:S(2)}) collective-permute-start(bf16[1,128,768]{2,1,0:T(8,128)(2,1)} %param.7), channel_id=1, source_target_pairs={{0,2},{1,3},{2,4},{3,5},{4,6},{5,7},{6,8},{7,9},{8,10},{9,11},{10,... | collective-permute-start | bytes 589832 | tf_op jit(solution)/shard_map/ppermute | solution.py:22
  5.5 18.4 %collective-permute-start.7 = (bf16[1,128,768]{2,1,0:T(8,128)(2,1)}, bf16[1,128,768]{2,1,0:T(8,128)(2,1)S(1)}, u32[]{:S(2)}, u32[]{:S(2)}) collective-permute-start(bf16[1,128,768]{2,1,0:T(8,128)(2,1)} %param.7), channel_id=1, source_target_pairs={{0,4},{1,5},{2,6},{3,7},{4,8},{5,9},{6,10},{7,11},{8,12},{9,13},{1... | collective-permute-start | bytes 589832 | tf_op jit(solution)/shard_map/ppermute | solution.py:22
  9.0 20.5 %collective-permute-start.4 = (bf16[1,128,768]{2,1,0:T(8,128)(2,1)}, bf16[1,128,768]{2,1,0:T(8,128)(2,1)}, u32[]{:S(2)}, u32[]{:S(2)}) collective-permute-start(bf16[1,128,768]{2,1,0:T(8,128)(2,1)} %param.7), channel_id=1, source_target_pairs={{4,0},{5,1},{6,2},{7,3},{8,4},{9,5},{10,6},{11,7},{12,8},{13,9},{1... | collective-permute-start | bytes 589832 | tf_op jit(solution)/shard_map/ppermute | solution.py:22
  10.3 24.5 %collective-permute-start.5 = (bf16[1,128,768]{2,1,0:T(8,128)(2,1)}, bf16[1,128,768]{2,1,0:T(8,128)(2,1)}, u32[]{:S(2)}, u32[]{:S(2)}) collective-permute-start(bf16[1,128,768]{2,1,0:T(8,128)(2,1)} %param.7), channel_id=1, source_target_pairs={{2,0},{3,1},{4,2},{5,3},{6,4},{7,5},{8,6},{9,7},{10,8},{11,9},{12,... | collective-permute-start | bytes 589832 | tf_op jit(solution)/shard_map/ppermute | solution.py:22
  20.7 3.2 %copy-start.3 = (bf16[1,128,768]{2,1,0:T(8,128)(2,1)}, bf16[1,128,768]{2,1,0:T(8,128)(2,1)S(1)}, u32[]{:S(2)}) copy-start(bf16[1,128,768]{2,1,0:T(8,128)(2,1)S(1)} %collective-permute-done.6) | copy-start | bytes 589828
  23.9 0.7 copy-start.1
  26.8 22.4 %copy-start = (bf16[1,128,1536]{2,1,0:T(8,128)(2,1)S(1)}, bf16[1,128,1536]{2,1,0:T(8,128)(2,1)}, u32[]{:S(2)}) copy-start(bf16[1,128,1536]{2,1,0:T(8,128)(2,1)} %param.4) | copy-start | bytes 1179652
  26.8 22.4 %copy-start.5 = (f32[1536]{0:T(1024)S(1)}, f32[1536]{0:T(1024)}, u32[]{:S(2)}) copy-start(f32[1536]{0:T(1024)} %param.5) | copy-start | bytes 18436
  29.6 14.4 %copy-start.2 = (bf16[1,128,768]{2,1,0:T(8,128)(2,1)S(1)}, bf16[1,128,768]{2,1,0:T(8,128)(2,1)}, u32[]{:S(2)}) copy-start(bf16[1,128,768]{2,1,0:T(8,128)(2,1)} %copy-done.1) | copy-start | bytes 589828
  40.1 9.2 %copy-start.4 = (bf16[1,128,768]{2,1,0:T(8,128)(2,1)S(1)}, bf16[1,128,768]{2,1,0:T(8,128)(2,1)}, u32[]{:S(2)}) copy-start(bf16[1,128,768]{2,1,0:T(8,128)(2,1)} %copy-done.3) | copy-start | bytes 589828
  53.7 58.8 %collective-permute-start = (bf16[1,128,1536]{2,1,0:T(8,128)(2,1)S(1)}, bf16[1,128,1536]{2,1,0:T(8,128)(2,1)S(1)}, u32[]{:S(2)}, u32[]{:S(2)}) collective-permute-start(bf16[1,128,1536]{2,1,0:T(8,128)(2,1)S(1)} %get-tuple-element.6), channel_id=1, source_target_pairs={{0,4},{1,5},{2,6},{3,7},{4,8},{5,9},{6,10},{7,11},{8,12},{9,13},{1... | collective-permute-start | bytes 1179656 | tf_op jit(solution)/shard_map/ppermute | solution.py:22
  59.2 56.6 %collective-permute-start.1 = (bf16[1,128,1536]{2,1,0:T(8,128)(2,1)S(1)}, bf16[1,128,1536]{2,1,0:T(8,128)(2,1)S(1)}, u32[]{:S(2)}, u32[]{:S(2)}) collective-permute-start(bf16[1,128,1536]{2,1,0:T(8,128)(2,1)S(1)} %get-tuple-element.6), channel_id=1, source_target_pairs={{0,2},{1,3},{2,4},{3,5},{4,6},{5,7},{6,8},{7,9},{8,10},{9,11},{10,... | collective-permute-start | bytes 1179656 | tf_op jit(solution)/shard_map/ppermute | solution.py:22
  62.8 56.4 %collective-permute-start.2 = (bf16[1,128,1536]{2,1,0:T(8,128)(2,1)S(1)}, bf16[1,128,1536]{2,1,0:T(8,128)(2,1)}, u32[]{:S(2)}, u32[]{:S(2)}) collective-permute-start(bf16[1,128,1536]{2,1,0:T(8,128)(2,1)S(1)} %get-tuple-element.6), channel_id=1, source_target_pairs={{2,0},{3,1},{4,2},{5,3},{6,4},{7,5},{8,6},{9,7},{10,8},{11,9},{12,... | collective-permute-start | bytes 1179656 | tf_op jit(solution)/shard_map/ppermute | solution.py:22
  64.1 64.1 %collective-permute-start.3 = (bf16[1,128,1536]{2,1,0:T(8,128)(2,1)S(1)}, bf16[1,128,1536]{2,1,0:T(8,128)(2,1)}, u32[]{:S(2)}, u32[]{:S(2)}) collective-permute-start(bf16[1,128,1536]{2,1,0:T(8,128)(2,1)S(1)} %get-tuple-element.6), channel_id=1, source_target_pairs={{4,0},{5,1},{6,2},{7,3},{8,4},{9,5},{10,6},{11,7},{12,8},{13,9},{1... | collective-permute-start | bytes 1179656 | tf_op jit(solution)/shard_map/ppermute | solution.py:22
